TPU v7x, 32 devices: a whole 2x2x4 slice. The times are simulated.
32 devices in a mesh: src: 8 (over z, y), tgt: 4 (over x, core).
Axes of the slice: x: 2, y: 2, z: 4, core: 2. Of those that a mesh axis runs over, the one named last changes fastest.
Arguments:
- sources: bfloat16 [8192, 512], P('src'), may hold values from -400 to 400
- log_src: float32 [8192], P('src'), may hold values from -1 to 1
- targets: bfloat16 [2048, 512], P(('src', 'tgt')), may hold values from -6 to 6
- potential: float32 [2048], P(('src', 'tgt')), may hold values from -5 to 5
- log_tgt: float32 [2048], P(('src', 'tgt')), may hold values from -1 to 1
Outputs:
- src_pot: float32 [8192], P('src')
- tgt_pot: float32 [2048], P(('src', 'tgt'))
- mapped: bfloat16 [8192, 512], P('src', 'tgt')
All inputs are finite; a program needn't handle non-finite values.
Results may differ from a plain program's by a relative error of at most 0.0144.
Values may be sent and summed in bfloat16 or wider, within the bound.
A program may use at most 64 MiB of HBM per device.

v0:
```python
import math

import jax
import jax.numpy as jnp
from jax import lax
from jax.sharding import PartitionSpec as P


def joined(value, axis, join):
    pieces = jax.tree.map(lambda part: lax.all_gather(part, axis), value)
    head = jax.tree.map(lambda part: part[0], pieces)
    tail = jax.tree.map(lambda part: part[1:], pieces)
    subtotal, _ = lax.scan(lambda subtotal, piece: (join(subtotal, piece), None), head, tail)
    return subtotal


def lse_pair(first, second):
    top = jnp.maximum(first[0], second[0])
    return (top, first[1] * jnp.exp(first[0] - top) + second[1] * jnp.exp(second[0] - top))


def scores_of(sources, piece, scale):
    product = lax.dot_general(
        sources, piece, (((1,), (1,)), ((), ())), preferred_element_type=jnp.float32
    )
    return product * scale


def body(sources, log_src, targets, potential, log_tgt):
    scale = 1.0 / math.sqrt(sources.shape[1])
    own = targets.shape[0]
    here = lax.axis_index("src") * own
    whole, pot_all, logt_all = (
        lax.all_gather(targets, "src", axis=0, tiled=True),
        lax.all_gather(potential.astype(jnp.bfloat16), "src", axis=0, tiled=True).astype(
            potential.dtype
        ),
        lax.all_gather(log_tgt.astype(jnp.bfloat16), "src", axis=0, tiled=True).astype(
            log_tgt.dtype
        ),
    )
    scores = scores_of(sources, whole, scale)
    shifted = scores + pot_all[None, :]
    row_top = jnp.max(shifted, axis=1)
    row_total = jnp.sum(jnp.exp(shifted - row_top[:, None]), axis=1)
    row_top, row_total = joined((row_top, row_total), "tgt", lse_pair)
    src_pot = log_src - (row_top + jnp.log(row_total))
    lifted = scores + src_pot[:, None]
    col_top = jnp.max(lifted, axis=0)
    col_total = jnp.sum(jnp.exp(lifted - col_top[None, :]), axis=0)
    peak, total = joined((col_top, col_total), "src", lse_pair)
    tgt_all = logt_all - (peak + jnp.log(total))
    tgt_pot = lax.dynamic_slice_in_dim(tgt_all, here, own)
    weight = jnp.exp(scores + src_pot[:, None] + tgt_all[None, :])
    mass_part = jnp.sum(weight, axis=1)
    moved = jnp.dot(weight.astype(jnp.bfloat16), whole, preferred_element_type=jnp.float32)
    mass = lax.psum(mass_part, "tgt")
    moved_mine = lax.psum_scatter(
        moved.astype(jnp.bfloat16), "tgt", scatter_dimension=1, tiled=True
    ).astype(jnp.float32)
    mapped = (moved_mine / mass[:, None]).astype(jnp.bfloat16)
    return (src_pot, tgt_pot, mapped)


def solution(mesh):
    placed = (
        P("src", None),
        P("src"),
        P(("src", "tgt"), None),
        P(("src", "tgt")),
        P(("src", "tgt")),
    )
    return jax.shard_map(
        body,
        mesh=mesh,
        in_specs=placed,
        out_specs=(P("src"), P(("src", "tgt")), P("src", "tgt")),
        check_vma=False,
    )
```

profile of v0, /device:TPU:0, one launch (start us, length us, event | category | flops | bytes accessed | tf_op | source)
XLA Modules:
  0.0 168.3 jit_solution(11736620196632521805)
XLA Ops:
  7.2 0.0 copy-start
  7.2 0.0 reduce-scatter.4.cloned.1.call-start
  7.2 0.7 convert_element_type.24
  8.0 0.7 convert_element_type.26
  8.6 1.2 dynamic-slice
  10.5 0.2 dynamic-update-slice
  10.8 0.2 dynamic-update-slice.1
  11.0 23.1 %all-reduce.2 = (bf16[512]{0:T(512)(128)(2,1)S(1)}, bf16[512]{0:T(512)(128)(2,1)S(1)}) all-reduce(bf16[512]{0:T(512)(128)(2,1)S(1)} %dynamic-update-slice, bf16[512]{0:T(512)(128)(2,1)S(1)} %dynamic-update-slice.1), channel_id=1, replica_groups=mesh['src'=8,'tgt'=4] {'src'}, use_global_device_ids=true, to_apply=%add | all-reduce | flops 1024 | bytes 4096
  34.1 31.7 %all_gather.33 = bf16[512,512]{1,0:T(8,128)(2,1)S(1)} all-gather(bf16[64,512]{1,0:T(8,128)(2,1)} %param.11), channel_id=1, replica_groups=mesh['src'=8,'tgt'=4] {'src'}, dimensions={0}, use_global_device_ids=true | all-gather | bytes 589824 | tf_op jit(solution)/shard_map/all_gather | solution.py:34
  65.9 0.0 copy-start.1
  65.9 0.8 copy-done.1
  66.7 0.0 copy-done
  66.7 0.7 add_reduce_fusion
  67.5 0.0 copy-start.3
  67.5 5.2 %all-gather = f32[4096]{0:T(1024)S(1)} all-gather(f32[1024]{0:T(1024)S(1)} %get-tuple-element.93), channel_id=2, replica_groups=mesh['src'=8,'tgt'=4] {'tgt'}, dimensions={0}, use_global_device_ids=true | all-gather | bytes 20480 | tf_op jit(solution)/shard_map/all_gather | solution.py:10
  72.7 0.5 exponential_reduce_fusion.1
  73.2 5.2 %all-gather.1 = f32[4096]{0:T(1024)S(1)} all-gather(f32[1024]{0:T(1024)S(1)} %exponential_reduce_fusion.1), channel_id=3, replica_groups=mesh['src'=8,'tgt'=4] {'tgt'}, dimensions={0}, use_global_device_ids=true | all-gather | bytes 20480 | tf_op jit(solution)/shard_map/all_gather | solution.py:10
  78.4 0.2 while.24
  78.6 0.0 copy-done.3
  78.6 0.0 copy-start.2
  78.6 0.3 fusion.2
  78.9 0.6 exponential_reduce_fusion
  79.4 26.1 %all-gather.5 = f32[8,1,512]{2,1,0:T(1,128)S(1)} all-gather(f32[1,1,512]{2,1,0:T(1,128)S(1)} %bitcast.39), channel_id=5, replica_groups=mesh['src'=8,'tgt'=4] {'src'}, dimensions={0}, use_global_device_ids=true | all-gather | bytes 18432 | tf_op jit(solution)/shard_map/all_gather | solution.py:10
  105.6 26.1 %all-gather.4 = f32[8,1,512]{2,1,0:T(1,128)S(1)} all-gather(f32[1,1,512]{2,1,0:T(1,128)S(1)} %bitcast.38), channel_id=4, replica_groups=mesh['src'=8,'tgt'=4] {'src'}, dimensions={0}, use_global_device_ids=true | all-gather | bytes 18432 | tf_op jit(solution)/shard_map/all_gather | solution.py:10
  131.7 0.4 while.25
  132.1 2.9 %convolution_convert_fusion = bf16[1024,512]{1,0:T(8,128)(2,1)} fusion(bf16[512,512]{1,0:T(8,128)(2,1)} %copy-done.1, f32[1024,512]{0,1:T(8,128)S(1)} %get-tuple-element.94, f32[512]{0:T(512)S(1)} %add_subtract_fusion.1, f32[1024]{0:T(1024)S(1)} %add_subtract_fusion), kind=kOutput, calls=%fused_computation.13 | convolution fusion | flops 539492352 | bytes 3676160 | tf_op jit(solution)/shard_map/dot_general | solution.py:56
  135.0 2.3 %copy.8 = bf16[1024,512]{0,1:T(8,128)(2,1)} copy(bf16[1024,512]{1,0:T(8,128)(2,1)} %convolution_convert_fusion) | data formatting | bytes 2097152
  137.3 0.0 reduce-scatter.4.cloned.1.call-update
  137.3 0.6 dynamic_slice.17
  137.9 0.0 copy-done.2
  137.9 0.5 fusion
  138.3 5.7 %psum.7 = f32[1024]{0:T(1024)S(1)} all-reduce(f32[1024]{0:T(1024)S(1)} %fusion), channel_id=1, replica_groups=mesh['src'=8,'tgt'=4] {'tgt'}, use_global_device_ids=true, to_apply=%region_10.11 | all-reduce | flops 1024 | bytes 8192 | tf_op jit(solution)/shard_map/psum | solution.py:57
  144.0 15.4 %reduce-scatter.4.cloned.1.call-done = bf16[128,1024]{1,0:T(8,128)(2,1)} async-done(((bf16[512,1024]{1,0:T(8,128)(2,1)}), bf16[128,1024]{1,0:T(8,128)(2,1)}) %reduce-scatter.4.cloned.1.call-update) | async-done | bytes 262160
  159.5 1.1 copy.9
  160.6 0.9 divide_convert_fusion
  (37 shorter events, 0.4 us)
Async XLA Ops:
  7.2 59.5 %copy-start = (bf16[1024,512]{1,0:T(8,128)(2,1)S(1)}, bf16[1024,512]{1,0:T(8,128)(2,1)}, u32[]{:S(2)}) copy-start(bf16[1024,512]{1,0:T(8,128)(2,1)} %param.9) | copy-start | bytes 3145732
  7.2 152.3 %reduce-scatter.4.cloned.1.call-start = ((), (), s32[]{:S(2)}) async-start(), calls=%async_computation.1 | async-start | bytes 1310720
  65.9 0.8 copy-start.1
  67.5 11.1 %copy-start.3 = (f32[1024]{0:T(1024)S(1)}, f32[1024]{0:T(1024)}, u32[]{:S(2)}) copy-start(f32[1024]{0:T(1024)} %param.10) | copy-start | bytes 12292
  78.6 59.3 %copy-start.2 = (f32[1024]{0:T(1024)}, f32[1024]{0:T(1024)S(1)}, u32[]{:S(2)}) copy-start(f32[1024]{0:T(1024)S(1)} %add_subtract_fusion) | copy-start | bytes 12292
Sparse Core Ops, SparseCore 0:
  137.4 22.0 reduce-scatter.3
where the time goes:
time: 169 us; the launch traced here: 168 us
  blocking collectives  123 us (73%)
  waiting for transfers between devices  15.5 us (9%)
  between operations  14.8 us (9%)
  local copies, waits for them, and re-layouts  6.68 us (4%)
  other arithmetic  4.3 us (3%)
  matrix products  3.64 us (2%)
    all_gather x4, blocking collectives, joined(): pieces = jax.tree.map(lambda part: lax.all_gather(part, axis), value)  62.6 us
    all_gather x1, blocking collectives, body(): lax.all_gather(targets, 'src', axis=0, tiled=True)  31.7 us
    unnamed x1, blocking collectives  23.1 us
    unnamed x2, waiting for transfers between devices  15.5 us
    unnamed x17, local copies, waits for them, and re-layouts  5.95 us
    psum x1, blocking collectives, body(): mass = lax.psum(mass_part, 'tgt')  5.67 us
  transfers between devices with their start and end apart: 1, of which 1 were waited for; matrix products, arithmetic and copies ran while one was open for 1% of the time, Pallas kernels for 0%

commit v1 on v0

v1 whole, which is shorter than its diff:
```python
import functools
import math

import jax
import jax.numpy as jnp
from jax import lax
from jax.experimental import pallas as pl
from jax.experimental.pallas import tpu as pltpu
from jax.sharding import PartitionSpec as P

MESH = pl.DeviceIdType.MESH
LANES = 128


def to_col(row):
    n = row.shape[1]
    eye = lax.broadcasted_iota(jnp.int32, (n, n), 0) == lax.broadcasted_iota(
        jnp.int32, (n, n), 1
    )
    return jnp.sum(jnp.where(eye, row, 0.0), axis=1, keepdims=True)


def to_row(col):
    n = col.shape[0]
    eye = lax.broadcasted_iota(jnp.int32, (n, n), 0) == lax.broadcasted_iota(
        jnp.int32, (n, n), 1
    )
    return jnp.sum(jnp.where(eye, col, 0.0), axis=0, keepdims=True)


def kernel(
    n_src, n_tgt, chunk,
    src_ref, lsrc_ref, tgt_ref, pot_ref, logt_ref,
    spot_ref, tpot_ref, out_ref,
    srcv, src_t, whole, whole_t, scores, q,
    aux, rstat, cstat, mstat, sendp, recvp, keep, sendx, recvx, logt_row, tgt_rows,
    lsem, zs, zr, fs, fr, aus, aur, rs, rr, cs, cr, ms, mr, ps, pr, xs, xr,
):
    s_me, t_me = lax.axis_index("src"), lax.axis_index("tgt")
    a_n, x_n = n_src // 2, n_tgt // 2
    a_me, b_me = s_me // 2, s_me % 2
    x_me, c_me = t_me // 2, t_me % 2
    rows, feats = src_ref.shape
    own = tgt_ref.shape[0]
    group = n_src * own
    half = a_n * own
    width = feats // n_tgt
    pieces = rows // chunk
    scale = 1.0 / math.sqrt(feats)
    slot_me = b_me * a_n + a_me

    def remote(src, dst, send, recv, s, t):
        return pltpu.make_async_remote_copy(
            src_ref=src, dst_ref=dst, send_sem=send, recv_sem=recv,
            device_id=(s, t), device_id_type=MESH,
        )

    load = pltpu.make_async_copy(src_ref, srcv, lsem)
    load.start()

    barrier = pltpu.get_barrier_semaphore()
    for d in range(1, n_src):
        pl.semaphore_signal(
            barrier, inc=1, device_id=((s_me + d) % n_src, t_me), device_id_type=MESH
        )
    for d in range(1, n_tgt):
        pl.semaphore_signal(
            barrier, inc=1, device_id=(s_me, (t_me + d) % n_tgt), device_id_type=MESH
        )
    aux[slot_me] = jnp.zeros(aux.shape[1:], aux.dtype)
    aux[slot_me, 0:1, 0:own] = pot_ref[...]
    aux[slot_me, 1:2, 0:own] = logt_ref[...]
    pl.semaphore_wait(barrier, n_src - 1 + n_tgt - 1)

    def rows_of(slot):
        return whole.at[pl.ds(pl.multiple_of(slot * own, own), own), :]

    sent = []
    order = [d for k in range(1, a_n // 2 + 1) for d in dict.fromkeys((k, a_n - k))]
    copy = remote(tgt_ref, rows_of(slot_me), fs.at[a_me], fr.at[a_me], s_me + 1 - 2 * b_me, t_me)
    copy.start()
    sent.append(copy)
    for d in order:
        a_to = (a_me + d) % a_n
        copy = remote(tgt_ref, rows_of(slot_me), zs.at[a_to], zr.at[a_me], a_to * 2 + b_me, t_me)
        copy.start()
        sent.append(copy)
    for d in range(1, n_src):
        s_to = (s_me + d) % n_src
        copy = remote(aux.at[slot_me], aux.at[slot_me], aus.at[s_to], aur.at[s_me], s_to, t_me)
        copy.start()
        sent.append(copy)
    mine = pltpu.make_async_copy(tgt_ref, rows_of(slot_me), zs.at[a_me])
    mine.start()

    load.wait()
    src_t[...] = srcv[...].T

    for d in range(1, n_src):
        s_from = (s_me + d) % n_src
        slot = (s_from % 2) * a_n + s_from // 2
        remote(aux.at[slot], aux.at[slot], aus.at[s_me], aur.at[s_from], s_from, t_me).wait_recv()

    mine.wait()
    for d in order:
        a_from = (a_me + d) % a_n
        slot = b_me * a_n + a_from
        remote(
            rows_of(slot), rows_of(slot), zs.at[a_me], zr.at[a_from], a_from * 2 + b_me, t_me
        ).wait_recv()
        copy = remote(
            rows_of(slot), rows_of(slot), fs.at[a_from], fr.at[a_from],
            s_me + 1 - 2 * b_me, t_me,
        )
        copy.start()
        sent.append(copy)

    def score_half(b):
        base = pl.multiple_of(b * half, half)
        points = whole[pl.ds(base, half), :]
        pot = jnp.concatenate(
            [to_col(aux[b * a_n + a, 0:1, 0:own]) for a in range(a_n)], axis=0
        )
        stats = []
        for k in range(pieces):
            cols = pl.ds(k * chunk, chunk)
            value = (
                jnp.dot(points, src_t[:, cols], preferred_element_type=jnp.float32) * scale
            )
            scores[pl.ds(base, half), cols] = value
            shifted = value + pot
            top = jnp.max(shifted, axis=0, keepdims=True)
            stats.append((top, jnp.sum(jnp.exp(shifted - top), axis=0, keepdims=True)))
        return stats

    first = score_half(b_me)
    for d in [0] + order:
        a_from = (a_me + d) % a_n
        slot = (1 - b_me) * a_n + a_from
        remote(
            rows_of(slot), rows_of(slot), fs.at[a_from], fr.at[a_from],
            s_me + 1 - 2 * b_me, t_me,
        ).wait_recv()
    second = score_half(1 - b_me)
    for k in range(pieces):
        cols = pl.ds(k * chunk, chunk)
        top = jnp.maximum(first[k][0], second[k][0])
        total = first[k][1] * jnp.exp(first[k][0] - top) + second[k][1] * jnp.exp(
            second[k][0] - top
        )
        rstat[t_me, 0:1, cols] = top
        rstat[t_me, 1:2, cols] = total
    for d in range(1, n_tgt):
        t_to = (t_me + d) % n_tgt
        copy = remote(rstat.at[t_me], rstat.at[t_me], rs.at[t_to], rr.at[t_me], s_me, t_to)
        copy.start()
        sent.append(copy)
    whole_t[...] = whole[...].T
    for slot in range(n_src):
        logt_row[0:1, pl.ds(slot * own, own)] = aux[slot, 1:2, 0:own]
    for d in range(1, n_tgt):
        t_from = (t_me + d) % n_tgt
        remote(
            rstat.at[t_from], rstat.at[t_from], rs.at[t_me], rr.at[t_from], s_me, t_from
        ).wait_recv()
    top = rstat[0, 0:1, :]
    for t in range(1, n_tgt):
        top = jnp.maximum(top, rstat[t, 0:1, :])
    total = rstat[0, 1:2, :] * jnp.exp(rstat[0, 0:1, :] - top)
    for t in range(1, n_tgt):
        total += rstat[t, 1:2, :] * jnp.exp(rstat[t, 0:1, :] - top)
    spot = lsrc_ref[...] - (top + jnp.log(total))
    spot_ref[...] = spot

    for j in range(group // LANES):
        lifted = scores[pl.ds(j * LANES, LANES), :] + spot
        top = jnp.max(lifted, axis=1, keepdims=True)
        e = jnp.exp(lifted - (top - 1.0))
        q[pl.ds(j * LANES, LANES), :] = e.astype(jnp.bfloat16)
        cstat[s_me, 0:1, pl.ds(j * LANES, LANES)] = to_row(top)
        cstat[s_me, 1:2, pl.ds(j * LANES, LANES)] = to_row(
            jnp.sum(e, axis=1, keepdims=True)
        )
    for d in range(1, n_src):
        s_to = (s_me + d) % n_src
        copy = remote(cstat.at[s_me], cstat.at[s_me], cs.at[s_to], cr.at[s_me], s_to, t_me)
        copy.start()
        sent.append(copy)
    for d in range(1, n_src):
        s_from = (s_me + d) % n_src
        remote(
            cstat.at[s_from], cstat.at[s_from], cs.at[s_me], cr.at[s_from], s_from, t_me
        ).wait_recv()
    peak = cstat[0, 0:1, :]
    for s in range(1, n_src):
        peak = jnp.maximum(peak, cstat[s, 0:1, :])
    total = cstat[0, 1:2, :] * jnp.exp(cstat[0, 0:1, :] - peak)
    for s in range(1, n_src):
        total += cstat[s, 1:2, :] * jnp.exp(cstat[s, 0:1, :] - peak)
    tgt_all = logt_row[...] - (peak + (jnp.log(total) - 1.0))
    factor = jnp.exp(cstat[s_me, 0:1, :] + tgt_all - 1.0)
    whole_t[...] = (whole_t[...].astype(jnp.float32) * factor).astype(jnp.bfloat16)

    def block(x, c, k):
        at = pl.multiple_of((x * 2 + c) * width, width)
        return jnp.dot(
            whole_t[pl.ds(at, width), :], q[:, pl.ds(k * chunk, chunk)],
            preferred_element_type=jnp.float32,
        )

    t_pair = x_me * 2 + 1 - c_me

    def to_partner(x, k):
        sendp[x, k] = block(x, 1 - c_me, k).astype(jnp.bfloat16)
        copy = remote(sendp.at[x, k], recvp.at[x, k], ps.at[x, k], pr.at[x, k], s_me, t_pair)
        copy.start()
        sent.append(copy)

    def from_partner(x, k):
        remote(
            sendp.at[x, k], recvp.at[x, k], ps.at[x, k], pr.at[x, k], s_me, t_pair
        ).wait_recv()

    others = [(x_me + d) % x_n for d in range(1, x_n)]
    for x in others:
        for k in range(pieces):
            to_partner(x, k)
    for x in others:
        for k in range(pieces):
            part = block(x, c_me, k)
            from_partner(x, k)
            sendx[x, k] = (part + recvp[x, k].astype(jnp.float32)).astype(jnp.bfloat16)
            copy = remote(
                sendx.at[x, k], recvx.at[x_me, k], xs.at[x, k], xr.at[x_me, k],
                s_me, x * 2 + c_me,
            )
            copy.start()
            sent.append(copy)
    high = factor.astype(jnp.bfloat16)
    low = (factor - high.astype(jnp.float32)).astype(jnp.bfloat16)
    which = lax.broadcasted_iota(jnp.int32, (16, group), 0)
    pair = jnp.where(
        which == 0, high.astype(jnp.float32),
        jnp.where(which == 1, low.astype(jnp.float32), 0.0),
    ).astype(jnp.bfloat16)
    for k in range(pieces):
        cols = pl.ds(k * chunk, chunk)
        both = jnp.dot(pair, q[:, cols], preferred_element_type=jnp.float32)
        mstat[t_me, 0:1, cols] = jnp.sum(both, axis=0, keepdims=True)
    for d in range(1, n_tgt):
        t_to = (t_me + d) % n_tgt
        copy = remote(mstat.at[t_me], mstat.at[t_me], ms.at[t_to], mr.at[t_me], s_me, t_to)
        copy.start()
        sent.append(copy)
    for k in range(pieces):
        to_partner(x_me, k)
    for k in range(pieces):
        keep[k] = block(x_me, c_me, k)
    for slot in range(n_src):
        tgt_rows[slot] = tgt_all[:, slot * own:(slot + 1) * own]
    tpot_ref[...] = tgt_rows[slot_me]
    for d in range(1, n_tgt):
        t_from = (t_me + d) % n_tgt
        remote(
            mstat.at[t_from], mstat.at[t_from], ms.at[t_me], mr.at[t_from], s_me, t_from
        ).wait_recv()
    mass = mstat[0]
    for t in range(1, n_tgt):
        mass += mstat[t]
    for k in range(pieces):
        from_partner(x_me, k)
        keep[k] += recvp[x_me, k].astype(jnp.float32)
    for k in range(pieces):
        value = keep[k]
        for x in others:
            remote(
                sendx.at[x, k], recvx.at[x, k], xs.at[x, k], xr.at[x, k],
                s_me, x * 2 + c_me,
            ).wait_recv()
            value += recvx[x, k].astype(jnp.float32)
        value = value / mass[:, k * chunk:(k + 1) * chunk]
        out_ref[pl.ds(k * chunk, chunk), :] = value.T.astype(jnp.bfloat16)
    for copy in sent:
        copy.wait_send()


def body(n_src, n_tgt, sources, log_src, targets, potential, log_tgt):
    rows, feats = sources.shape
    own = targets.shape[0]
    a_n, x_n = n_src // 2, n_tgt // 2
    group = n_src * own
    width = feats // n_tgt
    chunk = min(256, rows)
    pieces = rows // chunk
    f32, bf16 = jnp.float32, jnp.bfloat16
    dma = pltpu.SemaphoreType.DMA
    vmem = pl.BlockSpec(memory_space=pltpu.VMEM)
    hbm = pl.BlockSpec(memory_space=pl.ANY)
    padded = -(-own // LANES) * LANES
    spot, tpot, mapped = pl.pallas_call(
        functools.partial(kernel, n_src, n_tgt, chunk),
        name="sinkhorn",
        out_shape=(
            jax.ShapeDtypeStruct((1, rows), f32),
            jax.ShapeDtypeStruct((1, own), f32),
            jax.ShapeDtypeStruct((rows, width), bf16),
        ),
        in_specs=[hbm, vmem, hbm, vmem, vmem],
        out_specs=(vmem, vmem, vmem),
        scratch_shapes=[
            pltpu.VMEM((rows, feats), bf16),
            pltpu.VMEM((feats, rows), bf16),
            pltpu.VMEM((group, feats), bf16),
            pltpu.VMEM((feats, group), bf16),
            pltpu.VMEM((group, rows), f32),
            pltpu.VMEM((group, rows), bf16),
            pltpu.VMEM((n_src, 2, padded), f32),
            pltpu.VMEM((n_tgt, 2, rows), f32),
            pltpu.VMEM((n_src, 2, group), f32),
            pltpu.VMEM((n_tgt, 1, rows), f32),
            pltpu.VMEM((x_n, pieces, width, chunk), bf16),
            pltpu.VMEM((x_n, pieces, width, chunk), bf16),
            pltpu.VMEM((pieces, width, chunk), f32),
            pltpu.VMEM((x_n, pieces, width, chunk), bf16),
            pltpu.VMEM((x_n, pieces, width, chunk), bf16),
            pltpu.VMEM((1, group), f32),
            pltpu.VMEM((n_src, 1, own), f32),
            dma,
            dma((a_n,)), dma((a_n,)), dma((a_n,)), dma((a_n,)),
            dma((n_src,)), dma((n_src,)),
            dma((n_tgt,)), dma((n_tgt,)),
            dma((n_src,)), dma((n_src,)),
            dma((n_tgt,)), dma((n_tgt,)),
            dma((x_n, pieces)), dma((x_n, pieces)),
            dma((x_n, pieces)), dma((x_n, pieces)),
        ],
        compiler_params=pltpu.CompilerParams(
            collective_id=0, has_side_effects=True, vmem_limit_bytes=56 * 1024 * 1024
        ),
    )(
        sources, log_src.reshape(1, rows), targets,
        potential.reshape(1, own), log_tgt.reshape(1, own),
    )
    return spot.reshape(rows), tpot.reshape(own), mapped


def solution(mesh):
    placed = (
        P("src", None),
        P("src"),
        P(("src", "tgt"), None),
        P(("src", "tgt")),
        P(("src", "tgt")),
    )
    return jax.shard_map(
        functools.partial(body, mesh.shape["src"], mesh.shape["tgt"]),
        mesh=mesh,
        in_specs=placed,
        out_specs=(P("src"), P(("src", "tgt")), P("src", "tgt")),
        check_vma=False,
    )
```

time: 169 us -> 42.7 us (0.25)
  blocking collectives: 123 us -> 0 us
  Pallas kernels: 0 us -> 38.3 us
  waiting for transfers between devices: 15.5 us -> 0 us
  between operations: 14.8 us -> 0.65 us
  other arithmetic: 4.3 us -> 0 us
  matrix products: 3.64 us -> 0 us
  local copies, waits for them, and re-layouts: 6.68 us -> 3.52 us
    all_gather x5 -> x0, blocking collectives: 94.4 us -> none  [the longest x4 62.6 us: joined(): pieces = jax.tree.map(lambda part: lax.all_gather(part, axis), value)]
    pallas_call x0 -> x1, Pallas kernels: none -> 38.3 us  [body(): pl.pallas_call(functools.partial(kernel, n_src, n_tgt, chunk), name='sink...]
    unnamed x1 -> x0, blocking collectives: 23.1 us -> none
    unnamed x2 -> x0, waiting for transfers between devices: 15.5 us -> none
    psum x1 -> x0, blocking collectives: 5.67 us -> none  [body(): mass = lax.psum(mass_part, 'tgt')]
    dot_general x2 -> x0, matrix products: 3.64 us -> none  [the longest x1 2.89 us: body(): jnp.dot(weight.astype(jnp.bfloat16), whole, preferred_element_type=jnp.fl...]
    unnamed x17 -> x7, local copies, waits for them, and re-layouts: 5.95 us -> 3.52 us
    convert_element_type x4 -> x0, other arithmetic: 2.32 us -> none  [the longest x1 0.92 us: body(): mapped = (moved_mine / mass[:, None]).astype(jnp.bfloat16)]
  transfers between devices with their start and end apart: 1 -> 0, of which waited for: 1 -> 0; matrix products, arithmetic and copies ran while one was open for 1% -> 0% of each run, Pallas kernels for 0% -> 0%
where the time goes in v1:
time: 42.7 us; the launch traced here: 42.4 us
  Pallas kernels  38.3 us (90%)
  local copies, waits for them, and re-layouts  3.52 us (8%)
  between operations  0.65 us (2%)
    pallas_call x1, Pallas kernels, body(): pl.pallas_call(functools.partial(kernel, n_src, n_tgt, chunk), name='sink...  38.3 us
    unnamed x7, local copies, waits for them, and re-layouts  3.52 us

profile of v1, /device:TPU:0, one launch (start us, length us, event | category | flops | bytes accessed | tf_op | source)
XLA Modules:
  0.0 42.4 jit_solution(1636340015001345282)
XLA Ops:
  0.6 38.3 %sinkhorn.1 = (f32[1,1024]{1,0:T(1,128)}, f32[1,64]{1,0:T(1,128)}, bf16[1024,128]{1,0:T(8,128)(2,1)}) custom-call(bf16[1024,512]{1,0:T(8,128)(2,1)} %src_ref.1, f32[1,1024]{1,0:T(1,128)} %bitcast.5, bf16[64,512]{1,0:T(8,128)(2,1)} %tgt_ref.1, f32[1,64]{1,0:T(1,128)} %bitcast.7, f32[1,64]{1,0:T(1,128)} %bitcast.8), custom_call_target="tpu_custom_call" | custom-call | tf_op jit(solution)/shard_map/sinkhorn/pallas_call | solution.py:300
  38.9 0.0 copy-start
  38.9 0.7 %copy-done = f32[1,1024]{1,0:T(1,128)S(1)} copy-done((f32[1,1024]{1,0:T(1,128)S(1)}, f32[1,1024]{1,0:T(1,128)}, u32[]{:S(2)}) %copy-start) | copy-done | bytes 4120
  39.6 0.0 copy-start.1
  39.6 0.6 %copy.11 = f32[1024]{0:T(1024)} copy(f32[1024]{0:T(1024)S(1)} %bitcast.6) | data formatting | bytes 8192
  40.2 0.1 copy-done.1
  40.3 0.5 %copy.12 = f32[64]{0:T(128)} copy(f32[64]{0:T(128)S(1)} %bitcast.9) | data formatting | bytes 512
  40.8 1.7 %copy.13 = bf16[1024,128]{1,0:T(8,128)(2,1)} copy(bf16[1024,128]{1,0:T(8,128)(2,1)} %get-tuple-element.14) | data formatting | bytes 524288
Async XLA Ops:
  38.9 0.7 %copy-start = (f32[1,1024]{1,0:T(1,128)S(1)}, f32[1,1024]{1,0:T(1,128)}, u32[]{:S(2)}) copy-start(f32[1,1024]{1,0:T(1,128)} %get-tuple-element.6) | copy-start | bytes 12292
  39.6 0.7 %copy-start.1 = (f32[1,64]{1,0:T(1,128)S(1)}, f32[1,64]{1,0:T(1,128)}, u32[]{:S(2)}) copy-start(f32[1,64]{1,0:T(1,128)} %get-tuple-element.7) | copy-start | bytes 772

commit v2 on v1

--- a/solution.py
+++ b/solution.py
@@ -30,9 +30,9 @@
 
 def kernel(
     n_src, n_tgt, chunk,
-    src_ref, lsrc_ref, tgt_ref, pot_ref, logt_ref,
+    src_ref, lsrc_hbm, tgt_ref, pot_hbm, logt_hbm,
     spot_ref, tpot_ref, out_ref,
-    srcv, src_t, whole, whole_t, scores, q,
+    lsrc_ref, pot_ref, logt_ref, srcv, src_t, whole, whole_t, scores, q,
     aux, rstat, cstat, mstat, sendp, recvp, keep, sendx, recvx, logt_row, tgt_rows,
     lsem, zs, zr, fs, fr, aus, aur, rs, rr, cs, cr, ms, mr, ps, pr, xs, xr,
 ):
@@ -55,8 +55,15 @@
             device_id=(s, t), device_id_type=MESH,
         )
 
-    load = pltpu.make_async_copy(src_ref, srcv, lsem)
-    load.start()
+    slot_at = pl.ds(pl.multiple_of(slot_me * own, own), own)
+    mine = pltpu.make_async_copy(tgt_ref, whole.at[slot_at, :], zs.at[a_me])
+    mine.start()
+    small = [
+        pltpu.make_async_copy(source, target, lsem.at[1 + i])
+        for i, (source, target) in enumerate(
+            ((lsrc_hbm, lsrc_ref), (pot_hbm, pot_ref), (logt_hbm, logt_ref))
+        )
+    ]
 
     barrier = pltpu.get_barrier_semaphore()
     for d in range(1, n_src):
@@ -67,22 +74,36 @@
         pl.semaphore_signal(
             barrier, inc=1, device_id=(s_me, (t_me + d) % n_tgt), device_id_type=MESH
         )
+    for copy in small:
+        copy.start()
+    load = pltpu.make_async_copy(src_ref, srcv, lsem.at[0])
+    load.start()
+    for copy in small:
+        copy.wait()
     aux[slot_me] = jnp.zeros(aux.shape[1:], aux.dtype)
     aux[slot_me, 0:1, 0:own] = pot_ref[...]
     aux[slot_me, 1:2, 0:own] = logt_ref[...]
+    mine.wait()
     pl.semaphore_wait(barrier, n_src - 1 + n_tgt - 1)
 
     def rows_of(slot):
         return whole.at[pl.ds(pl.multiple_of(slot * own, own), own), :]
 
     sent = []
-    order = [d for k in range(1, a_n // 2 + 1) for d in dict.fromkeys((k, a_n - k))]
-    copy = remote(tgt_ref, rows_of(slot_me), fs.at[a_me], fr.at[a_me], s_me + 1 - 2 * b_me, t_me)
+    nearer = jnp.minimum(a_me, a_n - 1 - a_me)
+    side = jnp.where(a_me <= a_n - 1 - a_me, 1, -1)
+
+    def nth(k):
+        step = (k + 1) // 2 * (side if k % 2 else -side)
+        return a_me + jnp.where(k <= 2 * nearer, step, (k - nearer) * side)
+
+    order = list(range(a_n - 1, 0, -1))
+    copy = remote(rows_of(slot_me), rows_of(slot_me), fs.at[a_me], fr.at[a_me], s_me + 1 - 2 * b_me, t_me)
     copy.start()
     sent.append(copy)
     for d in order:
-        a_to = (a_me + d) % a_n
-        copy = remote(tgt_ref, rows_of(slot_me), zs.at[a_to], zr.at[a_me], a_to * 2 + b_me, t_me)
+        a_to = nth(d)
+        copy = remote(rows_of(slot_me), rows_of(slot_me), zs.at[a_to], zr.at[a_me], a_to * 2 + b_me, t_me)
         copy.start()
         sent.append(copy)
     for d in range(1, n_src):
@@ -90,30 +111,28 @@
         copy = remote(aux.at[slot_me], aux.at[slot_me], aus.at[s_to], aur.at[s_me], s_to, t_me)
         copy.start()
         sent.append(copy)
-    mine = pltpu.make_async_copy(tgt_ref, rows_of(slot_me), zs.at[a_me])
-    mine.start()
-
     load.wait()
-    src_t[...] = srcv[...].T
-
+    early = rows // 2
+    src_t[:, 0:early] = srcv[0:early, :].T
+
+    for d in order:
+        a_from = nth(d)
+        slot = b_me * a_n + a_from
+        remote(
+            rows_of(slot), rows_of(slot), zs.at[a_me], zr.at[a_from], a_from * 2 + b_me, t_me
+        ).wait_recv()
+        copy = remote(
+            rows_of(slot), rows_of(slot), fs.at[a_from], fr.at[a_from],
+            s_me + 1 - 2 * b_me, t_me,
+        )
+        copy.start()
+        sent.append(copy)
+
+    src_t[:, early:] = srcv[early:, :].T
     for d in range(1, n_src):
         s_from = (s_me + d) % n_src
         slot = (s_from % 2) * a_n + s_from // 2
         remote(aux.at[slot], aux.at[slot], aus.at[s_me], aur.at[s_from], s_from, t_me).wait_recv()
-
-    mine.wait()
-    for d in order:
-        a_from = (a_me + d) % a_n
-        slot = b_me * a_n + a_from
-        remote(
-            rows_of(slot), rows_of(slot), zs.at[a_me], zr.at[a_from], a_from * 2 + b_me, t_me
-        ).wait_recv()
-        copy = remote(
-            rows_of(slot), rows_of(slot), fs.at[a_from], fr.at[a_from],
-            s_me + 1 - 2 * b_me, t_me,
-        )
-        copy.start()
-        sent.append(copy)
 
     def score_half(b):
         base = pl.multiple_of(b * half, half)
@@ -284,6 +303,19 @@
         copy.wait_send()
 
 
+def finish(mapped_ref, spot_ref, tpot_ref, mapped_out, spot_out, tpot_out, sems):
+    copies = [
+        pltpu.make_async_copy(source, target, sems.at[i])
+        for i, (source, target) in enumerate(
+            ((mapped_ref, mapped_out), (spot_ref, spot_out), (tpot_ref, tpot_out))
+        )
+    ]
+    for copy in copies:
+        copy.start()
+    for copy in copies:
+        copy.wait()
+
+
 def body(n_src, n_tgt, sources, log_src, targets, potential, log_tgt):
     rows, feats = sources.shape
     own = targets.shape[0]
@@ -295,7 +327,7 @@
     f32, bf16 = jnp.float32, jnp.bfloat16
     dma = pltpu.SemaphoreType.DMA
     vmem = pl.BlockSpec(memory_space=pltpu.VMEM)
-    hbm = pl.BlockSpec(memory_space=pl.ANY)
+    hbm = pl.BlockSpec(memory_space=pltpu.HBM)
     padded = -(-own // LANES) * LANES
     spot, tpot, mapped = pl.pallas_call(
         functools.partial(kernel, n_src, n_tgt, chunk),
@@ -305,9 +337,12 @@
             jax.ShapeDtypeStruct((1, own), f32),
             jax.ShapeDtypeStruct((rows, width), bf16),
         ),
-        in_specs=[hbm, vmem, hbm, vmem, vmem],
+        in_specs=[hbm] * 5,
         out_specs=(vmem, vmem, vmem),
         scratch_shapes=[
+            pltpu.VMEM((1, rows), f32),
+            pltpu.VMEM((1, own), f32),
+            pltpu.VMEM((1, own), f32),
             pltpu.VMEM((rows, feats), bf16),
             pltpu.VMEM((feats, rows), bf16),
             pltpu.VMEM((group, feats), bf16),
@@ -325,7 +360,7 @@
             pltpu.VMEM((x_n, pieces, width, chunk), bf16),
             pltpu.VMEM((1, group), f32),
             pltpu.VMEM((n_src, 1, own), f32),
-            dma,
+            dma((4,)),
             dma((a_n,)), dma((a_n,)), dma((a_n,)), dma((a_n,)),
             dma((n_src,)), dma((n_src,)),
             dma((n_tgt,)), dma((n_tgt,)),
@@ -335,12 +370,30 @@
             dma((x_n, pieces)), dma((x_n, pieces)),
         ],
         compiler_params=pltpu.CompilerParams(
-            collective_id=0, has_side_effects=True, vmem_limit_bytes=56 * 1024 * 1024
+            collective_id=0, has_side_effects=True, vmem_limit_bytes=40 * 1024 * 1024
         ),
     )(
-        sources, log_src.reshape(1, rows), targets,
-        potential.reshape(1, own), log_tgt.reshape(1, own),
+        *(
+            pltpu.with_memory_space_constraint(array, pltpu.HBM)
+            for array in (
+                sources, log_src.reshape(1, rows), targets,
+                potential.reshape(1, own), log_tgt.reshape(1, own),
+            )
+        )
     )
+    mapped, spot, tpot = pl.pallas_call(
+        finish,
+        name="finish",
+        out_shape=(
+            jax.ShapeDtypeStruct((rows, width), bf16),
+            jax.ShapeDtypeStruct((1, rows), f32),
+            jax.ShapeDtypeStruct((1, own), f32),
+        ),
+        in_specs=[pl.BlockSpec(memory_space=pl.ANY)] * 3,
+        out_specs=(hbm,) * 3,
+        scratch_shapes=[dma((3,))],
+        compiler_params=pltpu.CompilerParams(vmem_limit_bytes=1024 * 1024),
+    )(mapped, spot, tpot)
     return spot.reshape(rows), tpot.reshape(own), mapped
 
 

time: 42.7 us -> 36.7 us (0.86)
  local copies, waits for them, and re-layouts: 3.52 us -> 0 us
  Pallas kernels: 38.3 us -> 35.9 us
    unnamed x7 -> x0, local copies, waits for them, and re-layouts: 3.52 us -> none
    pallas_call x1, Pallas kernels: 38.3 us -> 35.2 us  [body(): pl.pallas_call(functools.partial(kernel, n_src, n_tgt, chunk), name='sink...]
    pallas_call x0 -> x1, Pallas kernels: none -> 0.74 us  [body(): pl.pallas_call(finish, name='finish', out_shape=(jax.ShapeDtypeStruct((ro...]
where the time goes in v2:
time: 36.7 us; the launch traced here: 36.5 us
  Pallas kernels  35.9 us (98%)
  between operations  0.64 us (2%)
    pallas_call x1, Pallas kernels, body(): pl.pallas_call(functools.partial(kernel, n_src, n_tgt, chunk), name='sink...  35.2 us
    pallas_call x1, Pallas kernels, body(): pl.pallas_call(finish, name='finish', out_shape=(jax.ShapeDtypeStruct((ro...  0.74 us

profile of v2, /device:TPU:0, one launch (start us, length us, event | category | flops | bytes accessed | tf_op | source)
XLA Modules:
  0.0 36.5 jit_solution(8770260400930370860)
XLA Ops:
  0.6 35.2 %sinkhorn.1 = (f32[1,1024]{1,0:T(1,128)S(1)}, f32[1,64]{1,0:T(1,128)S(1)}, bf16[1024,128]{1,0:T(8,128)(2,1)S(1)}) custom-call(bf16[1024,512]{1,0:T(8,128)(2,1)} %src_ref.1, f32[1,1024]{1,0:T(1,128)} %bitcast.5, bf16[64,512]{1,0:T(8,128)(2,1)} %tgt_ref.1, f32[1,64]{1,0:T(1,128)} %bitcast.6, f32[1,64]{1,0:T(1,128)} %bitcast.7), custom_call_target="tpu_custom_call" | custom-call | tf_op jit(solution)/shard_map/sinkhorn/pallas_call | solution.py:332
  35.8 0.7 %finish.1 = (bf16[1024,128]{1,0:T(8,128)(2,1)}, f32[1,1024]{1,0:T(1,128)}, f32[1,64]{1,0:T(1,128)}) custom-call(bf16[1024,128]{1,0:T(8,128)(2,1)S(1)} %get-tuple-element.9.mapped_ref, f32[1,1024]{1,0:T(1,128)S(1)} %get-tuple-element.10.spot_ref, f32[1,64]{1,0:T(1,128)S(1)} %get-tuple-element.11.tpot_ref), custom_call_target="tpu_custom_call" | custom-call | tf_op jit(solution)/shard_map/finish/pallas_call | solution.py:384

commit v3 on v2

--- a/solution.py
+++ b/solution.py
@@ -28,12 +28,17 @@
     return jnp.sum(jnp.where(eye, col, 0.0), axis=0, keepdims=True)
 
 
+def joined(parts):
+    top = functools.reduce(jnp.maximum, parts)
+    return top + jnp.log(sum(jnp.exp(part - top) for part in parts))
+
+
 def kernel(
     n_src, n_tgt, chunk,
     src_ref, lsrc_hbm, tgt_ref, pot_hbm, logt_hbm,
     spot_ref, tpot_ref, out_ref,
     lsrc_ref, pot_ref, logt_ref, srcv, src_t, whole, whole_t, scores, q,
-    aux, rstat, cstat, mstat, sendp, recvp, keep, sendx, recvx, logt_row, tgt_rows,
+    aux, rstat, cstat, mstat, sendp, recvp, keep, sendx, recvx, logt_row, tops, tgt_rows,
     lsem, zs, zr, fs, fr, aus, aur, rs, rr, cs, cr, ms, mr, ps, pr, xs, xr,
 ):
     s_me, t_me = lax.axis_index("src"), lax.axis_index("tgt")
@@ -112,9 +117,6 @@
         copy.start()
         sent.append(copy)
     load.wait()
-    early = rows // 2
-    src_t[:, 0:early] = srcv[0:early, :].T
-
     for d in order:
         a_from = nth(d)
         slot = b_me * a_n + a_from
@@ -128,7 +130,7 @@
         copy.start()
         sent.append(copy)
 
-    src_t[:, early:] = srcv[early:, :].T
+    src_t[...] = srcv[...].T
     for d in range(1, n_src):
         s_from = (s_me + d) % n_src
         slot = (s_from % 2) * a_n + s_from // 2
@@ -167,9 +169,8 @@
         total = first[k][1] * jnp.exp(first[k][0] - top) + second[k][1] * jnp.exp(
             second[k][0] - top
         )
-        rstat[t_me, 0:1, cols] = top
-        rstat[t_me, 1:2, cols] = total
-    for d in range(1, n_tgt):
+        rstat[t_me, 0:1, cols] = top + jnp.log(total)
+    for d in [n_tgt // 2] + [d for d in range(1, n_tgt) if d != n_tgt // 2]:
         t_to = (t_me + d) % n_tgt
         copy = remote(rstat.at[t_me], rstat.at[t_me], rs.at[t_to], rr.at[t_me], s_me, t_to)
         copy.start()
@@ -182,13 +183,7 @@
         remote(
             rstat.at[t_from], rstat.at[t_from], rs.at[t_me], rr.at[t_from], s_me, t_from
         ).wait_recv()
-    top = rstat[0, 0:1, :]
-    for t in range(1, n_tgt):
-        top = jnp.maximum(top, rstat[t, 0:1, :])
-    total = rstat[0, 1:2, :] * jnp.exp(rstat[0, 0:1, :] - top)
-    for t in range(1, n_tgt):
-        total += rstat[t, 1:2, :] * jnp.exp(rstat[t, 0:1, :] - top)
-    spot = lsrc_ref[...] - (top + jnp.log(total))
+    spot = lsrc_ref[...] - joined([rstat[t] for t in range(n_tgt)])
     spot_ref[...] = spot
 
     for j in range(group // LANES):
@@ -196,12 +191,11 @@
         top = jnp.max(lifted, axis=1, keepdims=True)
         e = jnp.exp(lifted - (top - 1.0))
         q[pl.ds(j * LANES, LANES), :] = e.astype(jnp.bfloat16)
-        cstat[s_me, 0:1, pl.ds(j * LANES, LANES)] = to_row(top)
-        cstat[s_me, 1:2, pl.ds(j * LANES, LANES)] = to_row(
-            jnp.sum(e, axis=1, keepdims=True)
-        )
-    for d in range(1, n_src):
-        s_to = (s_me + d) % n_src
+        top, total = to_row(top), to_row(jnp.sum(e, axis=1, keepdims=True))
+        tops[0:1, pl.ds(j * LANES, LANES)] = top
+        cstat[s_me, 0:1, pl.ds(j * LANES, LANES)] = top + (jnp.log(total) - 1.0)
+    for a_to, flip in [(nth(k) if k else None, f) for k in order + [0] for f in (1, 0) if k or f]:
+        s_to = (a_me if a_to is None else a_to) * 2 + (1 - b_me if flip else b_me)
         copy = remote(cstat.at[s_me], cstat.at[s_me], cs.at[s_to], cr.at[s_me], s_to, t_me)
         copy.start()
         sent.append(copy)
@@ -210,14 +204,8 @@
         remote(
             cstat.at[s_from], cstat.at[s_from], cs.at[s_me], cr.at[s_from], s_from, t_me
         ).wait_recv()
-    peak = cstat[0, 0:1, :]
-    for s in range(1, n_src):
-        peak = jnp.maximum(peak, cstat[s, 0:1, :])
-    total = cstat[0, 1:2, :] * jnp.exp(cstat[0, 0:1, :] - peak)
-    for s in range(1, n_src):
-        total += cstat[s, 1:2, :] * jnp.exp(cstat[s, 0:1, :] - peak)
-    tgt_all = logt_row[...] - (peak + (jnp.log(total) - 1.0))
-    factor = jnp.exp(cstat[s_me, 0:1, :] + tgt_all - 1.0)
+    tgt_all = logt_row[...] - joined([cstat[s] for s in range(n_src)])
+    factor = jnp.exp(tops[...] + tgt_all - 1.0)
     whole_t[...] = (whole_t[...].astype(jnp.float32) * factor).astype(jnp.bfloat16)
 
     def block(x, c, k):
@@ -242,10 +230,11 @@
 
     others = [(x_me + d) % x_n for d in range(1, x_n)]
     for x in others:
-        for k in range(pieces):
-            to_partner(x, k)
+        to_partner(x, 0)
     for x in others:
         for k in range(pieces):
+            if k + 1 < pieces:
+                to_partner(x, k + 1)
             part = block(x, c_me, k)
             from_partner(x, k)
             sendx[x, k] = (part + recvp[x, k].astype(jnp.float32)).astype(jnp.bfloat16)
@@ -322,7 +311,7 @@
     a_n, x_n = n_src // 2, n_tgt // 2
     group = n_src * own
     width = feats // n_tgt
-    chunk = min(256, rows)
+    chunk = min(512, rows)
     pieces = rows // chunk
     f32, bf16 = jnp.float32, jnp.bfloat16
     dma = pltpu.SemaphoreType.DMA
@@ -350,14 +339,15 @@
             pltpu.VMEM((group, rows), f32),
             pltpu.VMEM((group, rows), bf16),
             pltpu.VMEM((n_src, 2, padded), f32),
-            pltpu.VMEM((n_tgt, 2, rows), f32),
-            pltpu.VMEM((n_src, 2, group), f32),
+            pltpu.VMEM((n_tgt, 1, rows), f32),
+            pltpu.VMEM((n_src, 1, group), f32),
             pltpu.VMEM((n_tgt, 1, rows), f32),
             pltpu.VMEM((x_n, pieces, width, chunk), bf16),
             pltpu.VMEM((x_n, pieces, width, chunk), bf16),
             pltpu.VMEM((pieces, width, chunk), f32),
             pltpu.VMEM((x_n, pieces, width, chunk), bf16),
             pltpu.VMEM((x_n, pieces, width, chunk), bf16),
+            pltpu.VMEM((1, group), f32),
             pltpu.VMEM((1, group), f32),
             pltpu.VMEM((n_src, 1, own), f32),
             dma((4,)),

time: 36.7 us -> 36 us (0.981)
  Pallas kernels: 35.9 us -> 35.2 us
    pallas_call x1, Pallas kernels: 35.2 us -> 34.5 us  [body(): pl.pallas_call(functools.partial(kernel, n_src, n_tgt, chunk), name='sink...]
where the time goes in v3:
time: 36 us; the launch traced here: 35.9 us
  Pallas kernels  35.2 us (98%)
  between operations  0.64 us (2%)
    pallas_call x1, Pallas kernels, body(): pl.pallas_call(functools.partial(kernel, n_src, n_tgt, chunk), name='sink...  34.5 us
    pallas_call x1, Pallas kernels, body(): pl.pallas_call(finish, name='finish', out_shape=(jax.ShapeDtypeStruct((ro...  0.74 us

profile of v3, /device:TPU:0, one launch (start us, length us, event | category | flops | bytes accessed | tf_op | source)
XLA Modules:
  0.0 35.9 jit_solution(5380689946588460671)
XLA Ops:
  0.6 34.5 %sinkhorn.1 = (f32[1,1024]{1,0:T(1,128)S(1)}, f32[1,64]{1,0:T(1,128)S(1)}, bf16[1024,128]{1,0:T(8,128)(2,1)S(1)}) custom-call(bf16[1024,512]{1,0:T(8,128)(2,1)} %src_ref.1, f32[1,1024]{1,0:T(1,128)} %bitcast.5, bf16[64,512]{1,0:T(8,128)(2,1)} %tgt_ref.1, f32[1,64]{1,0:T(1,128)} %bitcast.6, f32[1,64]{1,0:T(1,128)} %bitcast.7), custom_call_target="tpu_custom_call" | custom-call | tf_op jit(solution)/shard_map/sinkhorn/pallas_call | solution.py:321
  35.1 0.7 %finish.1 = (bf16[1024,128]{1,0:T(8,128)(2,1)}, f32[1,1024]{1,0:T(1,128)}, f32[1,64]{1,0:T(1,128)}) custom-call(bf16[1024,128]{1,0:T(8,128)(2,1)S(1)} %get-tuple-element.9.mapped_ref, f32[1,1024]{1,0:T(1,128)S(1)} %get-tuple-element.10.spot_ref, f32[1,64]{1,0:T(1,128)S(1)} %get-tuple-element.11.tpot_ref), custom_call_target="tpu_custom_call" | custom-call | tf_op jit(solution)/shard_map/finish/pallas_call | solution.py:374

commit v4 on v3

--- a/solution.py
+++ b/solution.py
@@ -206,12 +206,12 @@
         ).wait_recv()
     tgt_all = logt_row[...] - joined([cstat[s] for s in range(n_src)])
     factor = jnp.exp(tops[...] + tgt_all - 1.0)
-    whole_t[...] = (whole_t[...].astype(jnp.float32) * factor).astype(jnp.bfloat16)
 
     def block(x, c, k):
         at = pl.multiple_of((x * 2 + c) * width, width)
+        points = (whole_t[pl.ds(at, width), :].astype(jnp.float32) * factor).astype(jnp.bfloat16)
         return jnp.dot(
-            whole_t[pl.ds(at, width), :], q[:, pl.ds(k * chunk, chunk)],
+            points, q[:, pl.ds(k * chunk, chunk)],
             preferred_element_type=jnp.float32,
         )
 
@@ -231,6 +231,22 @@
     others = [(x_me + d) % x_n for d in range(1, x_n)]
     for x in others:
         to_partner(x, 0)
+    high = factor.astype(jnp.bfloat16)
+    low = (factor - high.astype(jnp.float32)).astype(jnp.bfloat16)
+    which = lax.broadcasted_iota(jnp.int32, (16, group), 0)
+    pair = jnp.where(
+        which == 0, high.astype(jnp.float32),
+        jnp.where(which == 1, low.astype(jnp.float32), 0.0),
+    ).astype(jnp.bfloat16)
+    for k in range(pieces):
+        cols = pl.ds(k * chunk, chunk)
+        both = jnp.dot(pair, q[:, cols], preferred_element_type=jnp.float32)
+        mstat[t_me, 0:1, cols] = jnp.sum(both, axis=0, keepdims=True)
+    for d in range(1, n_tgt):
+        t_to = (t_me + d) % n_tgt
+        copy = remote(mstat.at[t_me], mstat.at[t_me], ms.at[t_to], mr.at[t_me], s_me, t_to)
+        copy.start()
+        sent.append(copy)
     for x in others:
         for k in range(pieces):
             if k + 1 < pieces:
@@ -244,22 +260,6 @@
             )
             copy.start()
             sent.append(copy)
-    high = factor.astype(jnp.bfloat16)
-    low = (factor - high.astype(jnp.float32)).astype(jnp.bfloat16)
-    which = lax.broadcasted_iota(jnp.int32, (16, group), 0)
-    pair = jnp.where(
-        which == 0, high.astype(jnp.float32),
-        jnp.where(which == 1, low.astype(jnp.float32), 0.0),
-    ).astype(jnp.bfloat16)
-    for k in range(pieces):
-        cols = pl.ds(k * chunk, chunk)
-        both = jnp.dot(pair, q[:, cols], preferred_element_type=jnp.float32)
-        mstat[t_me, 0:1, cols] = jnp.sum(both, axis=0, keepdims=True)
-    for d in range(1, n_tgt):
-        t_to = (t_me + d) % n_tgt
-        copy = remote(mstat.at[t_me], mstat.at[t_me], ms.at[t_to], mr.at[t_me], s_me, t_to)
-        copy.start()
-        sent.append(copy)
     for k in range(pieces):
         to_partner(x_me, k)
     for k in range(pieces):

time: 36 us -> 35.4 us (0.983)
  Pallas kernels: 35.2 us -> 34.6 us
    pallas_call x1, Pallas kernels: 34.5 us -> 33.9 us  [body(): pl.pallas_call(functools.partial(kernel, n_src, n_tgt, chunk), name='sink...]
where the time goes in v4:
time: 35.4 us; the launch traced here: 35.2 us
  Pallas kernels  34.6 us (98%)
  between operations  0.64 us (2%)
    pallas_call x1, Pallas kernels, body(): pl.pallas_call(functools.partial(kernel, n_src, n_tgt, chunk), name='sink...  33.9 us
    pallas_call x1, Pallas kernels, body(): pl.pallas_call(finish, name='finish', out_shape=(jax.ShapeDtypeStruct((ro...  0.74 us

profile of v4, /device:TPU:0, one launch (start us, length us, event | category | flops | bytes accessed | tf_op | source)
XLA Modules:
  0.0 35.2 jit_solution(10785743151491083520)
XLA Ops:
  0.6 33.9 %sinkhorn.1 = (f32[1,1024]{1,0:T(1,128)S(1)}, f32[1,64]{1,0:T(1,128)S(1)}, bf16[1024,128]{1,0:T(8,128)(2,1)S(1)}) custom-call(bf16[1024,512]{1,0:T(8,128)(2,1)} %src_ref.1, f32[1,1024]{1,0:T(1,128)} %bitcast.5, bf16[64,512]{1,0:T(8,128)(2,1)} %tgt_ref.1, f32[1,64]{1,0:T(1,128)} %bitcast.6, f32[1,64]{1,0:T(1,128)} %bitcast.7), custom_call_target="tpu_custom_call" | custom-call | tf_op jit(solution)/shard_map/sinkhorn/pallas_call | solution.py:321
  34.5 0.7 %finish.1 = (bf16[1024,128]{1,0:T(8,128)(2,1)}, f32[1,1024]{1,0:T(1,128)}, f32[1,64]{1,0:T(1,128)}) custom-call(bf16[1024,128]{1,0:T(8,128)(2,1)S(1)} %get-tuple-element.9.mapped_ref, f32[1,1024]{1,0:T(1,128)S(1)} %get-tuple-element.10.spot_ref, f32[1,64]{1,0:T(1,128)S(1)} %get-tuple-element.11.tpot_ref), custom_call_target="tpu_custom_call" | custom-call | tf_op jit(solution)/shard_map/finish/pallas_call | solution.py:374
